TPU v7x, 256 devices: a whole 4x4x8 slice. The times are simulated.
256 devices in a mesh: gx: 32 (over x, z), gy: 8 (over y, core).
Axes of the slice: x: 4, y: 4, z: 8, core: 2. Of those that a mesh axis runs over, the one named last changes fastest.
Arguments:
- flow_state: float32 [4, 4096, 1024], P(None, 'gx', 'gy'), may hold values from -6 to 6
- sound_speed_sq: float32 [4096, 1024], P('gx', 'gy'), may hold values from 0.25 to 1
- snapshots: bfloat16 [62, 4096, 1024], P(None, 'gx', 'gy'), may hold values from -96 to 96
Outputs:
- new_state: float32 [4, 4096, 1024], P(None, 'gx', 'gy')
- pod_basis: float32 [64, 4096, 1024], P(None, 'gx', 'gy')
All inputs are finite; a program needn't handle non-finite values.
Results may differ from a plain program's by a relative error of at most 0.00063.
Values sent between devices are 32-bit elements; how exact they have to be, the bound alone decides.
A program may use at most 64 MiB of HBM per device.

v0:
```python
import jax
import jax.numpy as jnp
from jax import lax
from jax.sharding import PartitionSpec as P

STEPS = 2
courant = 0.8
stream_speed = 0.3
span_speed = 0.1


def padded_2(block, sides, width):
    for axis, dim in sides:
        count = lax.axis_size(axis)
        forward = [(i, i + 1) for i in range(count - 1)]
        forward.append((count - 1, 0))
        backward = [(target, source) for source, target in forward]
        low = lax.ppermute(
            lax.slice_in_dim(block, block.shape[dim] - width, None, axis=dim), axis, forward
        )
        high = lax.ppermute(lax.slice_in_dim(block, 0, width, axis=dim), axis, backward)
        block = jnp.concatenate([low, block, high], axis=dim)
    return block


def derivative_x(padded):
    interior = padded[:, :, 2:-2]
    extent = interior.shape[1] - 4
    ahead_one = interior[:, 3 : 3 + extent]
    behind_one = interior[:, 1 : 1 + extent]
    ahead_two = interior[:, 4 : 4 + extent]
    behind_two = interior[:, 0:extent]
    return (8.0 * (ahead_one - behind_one) - (ahead_two - behind_two)) / 12.0


def derivative_y(padded):
    interior = padded[:, 2:-2, :]
    extent = interior.shape[2] - 4
    ahead_one = interior[:, :, 3 : 3 + extent]
    behind_one = interior[:, :, 1 : 1 + extent]
    ahead_two = interior[:, :, 4 : 4 + extent]
    behind_two = interior[:, :, 0:extent]
    return (8.0 * (ahead_one - behind_one) - (ahead_two - behind_two)) / 12.0


def tendency(padded, sound_sq):
    slope_x = derivative_x(padded)
    slope_y = derivative_y(padded)
    advect = stream_speed * slope_x + span_speed * slope_y
    diverge = slope_x[1] + slope_y[2]
    rate_rho = -courant * (advect[0] + diverge)
    rate_mx = -courant * (advect[1] + slope_x[3])
    rate_my = -courant * (advect[2] + slope_y[3])
    rate_p = -courant * (advect[3] + sound_sq * diverge)
    return jnp.stack([rate_rho, rate_mx, rate_my, rate_p])


def extend(current):
    return padded_2(current, (("gx", 1), ("gy", 2)), 2)


def advance(current, sound_sq):
    first = current + tendency(extend(current), sound_sq)
    second = 0.75 * current + 0.25 * (first + tendency(extend(first), sound_sq))
    return 1.0 / 3.0 * current + 2.0 / 3.0 * (second + tendency(extend(second), sound_sq))


def body(flow_state, sound_speed_sq, snapshots):
    current = flow_state
    columns = [snapshots]
    for step_index in range(STEPS):
        current = advance(current, sound_speed_sq)
        columns.append(current[3].astype(jnp.bfloat16)[None])
    snap_block = jnp.concatenate(columns, axis=0)
    mode_count = snap_block.shape[0]
    flat_block = snap_block.reshape(mode_count, -1)
    cell_total = flat_block.shape[1] * lax.axis_size("gx") * lax.axis_size("gy")
    local_gram = (
        lax.dot_general(
            flat_block, flat_block, (((1,), (1,)), ((), ())), preferred_element_type=jnp.float32
        )
        / cell_total
    )
    gram = lax.psum(local_gram, ("gx", "gy"))
    lower_factor = jnp.linalg.cholesky(gram)
    identity_matrix = jnp.eye(mode_count, dtype=jnp.float32)
    inverse = jax.scipy.linalg.solve_triangular(lower_factor, identity_matrix, lower=True)
    pod_basis = jnp.dot(inverse, flat_block.astype(jnp.float32), precision=lax.Precision.HIGHEST)
    return (current, pod_basis.reshape(snap_block.shape))


def solution(mesh):
    placed = (P(None, "gx", "gy"), P("gx", "gy"), P(None, "gx", "gy"))
    return jax.shard_map(
        body,
        mesh=mesh,
        in_specs=placed,
        out_specs=(P(None, "gx", "gy"), P(None, "gx", "gy")),
        check_vma=False,
    )
```

profile of v0, /device:TPU:1, one launch (start us, length us, event | category | flops | bytes accessed | tf_op | source)
XLA Modules:
  0.0 197.1 jit_solution(15976753331273612163)
XLA Ops:
  1.4 2.5 %collective-permute-start.1 = (f32[4,2,128]{2,1,0:T(2,128)S(1)}, f32[4,2,128]{2,1,0:T(2,128)S(1)}, u32[]{:S(2)}, u32[]{:S(2)}) collective-permute-start(f32[4,2,128]{2,1,0:T(2,128)S(1)} %get-tuple-element.73), channel_id=1, source_target_pairs={{0,8},{8,16},{16,24},{24,32},{32,40},{40,48},{48,56},{56,64},{64,7... | collective-permute-start | bytes 12296 | tf_op jit(solution)/shard_map/ppermute | solution.py:18
  3.9 6.2 %collective-permute-start = (f32[4,2,128]{2,1,0:T(2,128)S(1)}, f32[4,2,128]{2,1,0:T(2,128)S(1)}, u32[]{:S(2)}, u32[]{:S(2)}) collective-permute-start(f32[4,2,128]{2,1,0:T(2,128)S(1)} %get-tuple-element.74), channel_id=1, source_target_pairs={{8,0},{16,8},{24,16},{32,24},{40,32},{48,40},{56,48},{64,56},{72,6... | collective-permute-start | bytes 12296 | tf_op jit(solution)/shard_map/ppermute | solution.py:21
  14.9 4.5 %collective-permute-done.2 = f32[4,132,2]{2,1,0:T(8,128)S(1)} collective-permute-done((f32[4,132,2]{2,1,0:T(8,128)S(1)}, f32[4,132,2]{2,1,0:T(8,128)S(1)}, u32[]{:S(2)}, u32[]{:S(2)}) %collective-permute-start.2) | collective-permute-done | bytes 4256 | tf_op jit(solution)/shard_map/ppermute | solution.py:21
  19.4 2.0 %broadcast_multiply_fusion.10 = (f32[4,128,128]{2,1,0:T(8,128)S(1)}, f32[4,128,128]{2,1,0:T(8,128)S(1)}, f32[4,130,128]{2,1,0:T(8,128)S(1)}) fusion(f32[4,2,128]{2,1,0:T(2,128)S(1)} %collective-permute-done, f32[4,128,128]{2,1,0:T(8,128)} %param.3, f32[4,2,128]{2,1,0:T(2,128)S(1)} %collective-permute-done.1, f32[4,132,2]{2,1,0:T(8,128)S(1)} %collective-permute-done.3, ...), kind=kLoop, calls=%fused_computation.177 | loop fusion | flops 1114111 | bytes 1065216 | tf_op jit(solution)/shard_map/div | solution.py:43
  21.8 5.2 %collective-permute-start.4 = (f32[4,2,128]{2,1,0:T(2,128)S(1)}, f32[4,2,128]{2,1,0:T(2,128)S(1)}, u32[]{:S(2)}, u32[]{:S(2)}) collective-permute-start(f32[4,2,128]{2,1,0:T(2,128)S(1)} %get-tuple-element.71), channel_id=1, source_target_pairs={{8,0},{16,8},{24,16},{32,24},{40,32},{48,40},{56,48},{64,56},{72,6... | collective-permute-start | bytes 12296 | tf_op jit(solution)/shard_map/ppermute | solution.py:21
  28.1 3.9 %collective-permute-start.6 = (f32[4,132,2]{2,1,0:T(8,128)S(1)}, f32[4,132,2]{2,1,0:T(8,128)S(1)}, u32[]{:S(2)}, u32[]{:S(2)}) collective-permute-start(f32[4,132,2]{2,1,0:T(8,128)S(1)} %get-tuple-element.58), channel_id=1, source_target_pairs={{1,0},{2,1},{3,2},{4,3},{5,4},{6,5},{7,6},{0,7},{9,8},{10,9},{11,1... | collective-permute-start | bytes 12680 | tf_op jit(solution)/shard_map/ppermute | solution.py:21
  32.1 2.6 %collective-permute-done.6 = f32[4,132,2]{2,1,0:T(8,128)S(1)} collective-permute-done((f32[4,132,2]{2,1,0:T(8,128)S(1)}, f32[4,132,2]{2,1,0:T(8,128)S(1)}, u32[]{:S(2)}, u32[]{:S(2)}) %collective-permute-start.6) | collective-permute-done | bytes 4256 | tf_op jit(solution)/shard_map/ppermute | solution.py:21
  36.3 5.1 %collective-permute-start.8 = (f32[4,2,128]{2,1,0:T(2,128)S(1)}, f32[4,2,128]{2,1,0:T(2,128)S(1)}, u32[]{:S(2)}, u32[]{:S(2)}) collective-permute-start(f32[4,2,128]{2,1,0:T(2,128)S(1)} %get-tuple-element.69), channel_id=1, source_target_pairs={{8,0},{16,8},{24,16},{32,24},{40,32},{48,40},{56,48},{64,56},{72,6... | collective-permute-start | bytes 12296 | tf_op jit(solution)/shard_map/ppermute | solution.py:21
  42.6 4.6 %collective-permute-start.10 = (f32[4,132,2]{2,1,0:T(8,128)S(1)}, f32[4,132,2]{2,1,0:T(8,128)S(1)}, u32[]{:S(2)}, u32[]{:S(2)}) collective-permute-start(f32[4,132,2]{2,1,0:T(8,128)S(1)} %get-tuple-element.56), channel_id=1, source_target_pairs={{1,0},{2,1},{3,2},{4,3},{5,4},{6,5},{7,6},{0,7},{9,8},{10,9},{11,1... | collective-permute-start | bytes 12680 | tf_op jit(solution)/shard_map/ppermute | solution.py:21
  47.3 2.9 %collective-permute-done.10 = f32[4,132,2]{2,1,0:T(8,128)S(1)} collective-permute-done((f32[4,132,2]{2,1,0:T(8,128)S(1)}, f32[4,132,2]{2,1,0:T(8,128)S(1)}, u32[]{:S(2)}, u32[]{:S(2)}) %collective-permute-start.10) | collective-permute-done | bytes 4256 | tf_op jit(solution)/shard_map/ppermute | solution.py:21
  51.5 5.2 %collective-permute-start.12 = (f32[4,2,128]{2,1,0:T(2,128)S(1)}, f32[4,2,128]{2,1,0:T(2,128)S(1)}, u32[]{:S(2)}, u32[]{:S(2)}) collective-permute-start(f32[4,2,128]{2,1,0:T(2,128)S(1)} %get-tuple-element.67), channel_id=1, source_target_pairs={{8,0},{16,8},{24,16},{32,24},{40,32},{48,40},{56,48},{64,56},{72,6... | collective-permute-start | bytes 12296 | tf_op jit(solution)/shard_map/ppermute | solution.py:21
  57.9 4.6 %collective-permute-start.14 = (f32[4,132,2]{2,1,0:T(8,128)S(1)}, f32[4,132,2]{2,1,0:T(8,128)S(1)}, u32[]{:S(2)}, u32[]{:S(2)}) collective-permute-start(f32[4,132,2]{2,1,0:T(8,128)S(1)} %get-tuple-element.54), channel_id=1, source_target_pairs={{1,0},{2,1},{3,2},{4,3},{5,4},{6,5},{7,6},{0,7},{9,8},{10,9},{11,1... | collective-permute-start | bytes 12680 | tf_op jit(solution)/shard_map/ppermute | solution.py:21
  62.6 2.9 %collective-permute-done.14 = f32[4,132,2]{2,1,0:T(8,128)S(1)} collective-permute-done((f32[4,132,2]{2,1,0:T(8,128)S(1)}, f32[4,132,2]{2,1,0:T(8,128)S(1)}, u32[]{:S(2)}, u32[]{:S(2)}) %collective-permute-start.14) | collective-permute-done | bytes 4256 | tf_op jit(solution)/shard_map/ppermute | solution.py:21
  66.8 5.4 %collective-permute-start.16 = (f32[4,2,128]{2,1,0:T(2,128)S(1)}, f32[4,2,128]{2,1,0:T(2,128)S(1)}, u32[]{:S(2)}, u32[]{:S(2)}) collective-permute-start(f32[4,2,128]{2,1,0:T(2,128)S(1)} %get-tuple-element.65), channel_id=1, source_target_pairs={{8,0},{16,8},{24,16},{32,24},{40,32},{48,40},{56,48},{64,56},{72,6... | collective-permute-start | bytes 12296 | tf_op jit(solution)/shard_map/ppermute | solution.py:21
  75.4 4.0 %collective-permute-start.18 = (f32[4,132,2]{2,1,0:T(8,128)S(1)}, f32[4,132,2]{2,1,0:T(8,128)S(1)}, u32[]{:S(2)}, u32[]{:S(2)}) collective-permute-start(f32[4,132,2]{2,1,0:T(8,128)S(1)} %get-tuple-element.52), channel_id=1, source_target_pairs={{1,0},{2,1},{3,2},{4,3},{5,4},{6,5},{7,6},{0,7},{9,8},{10,9},{11,1... | collective-permute-start | bytes 12680 | tf_op jit(solution)/shard_map/ppermute | solution.py:21
  79.5 2.9 %collective-permute-done.18 = f32[4,132,2]{2,1,0:T(8,128)S(1)} collective-permute-done((f32[4,132,2]{2,1,0:T(8,128)S(1)}, f32[4,132,2]{2,1,0:T(8,128)S(1)}, u32[]{:S(2)}, u32[]{:S(2)}) %collective-permute-start.18) | collective-permute-done | bytes 4256 | tf_op jit(solution)/shard_map/ppermute | solution.py:21
  83.7 4.8 %collective-permute-start.20 = (f32[4,2,128]{2,1,0:T(2,128)S(1)}, f32[4,2,128]{2,1,0:T(2,128)S(1)}, u32[]{:S(2)}, u32[]{:S(2)}) collective-permute-start(f32[4,2,128]{2,1,0:T(2,128)S(1)} %get-tuple-element.63), channel_id=1, source_target_pairs={{8,0},{16,8},{24,16},{32,24},{40,32},{48,40},{56,48},{64,56},{72,6... | collective-permute-start | bytes 12296 | tf_op jit(solution)/shard_map/ppermute | solution.py:21
  89.7 4.9 %collective-permute-start.22 = (f32[4,132,2]{2,1,0:T(8,128)S(1)}, f32[4,132,2]{2,1,0:T(8,128)S(1)}, u32[]{:S(2)}, u32[]{:S(2)}) collective-permute-start(f32[4,132,2]{2,1,0:T(8,128)S(1)} %get-tuple-element.50), channel_id=1, source_target_pairs={{1,0},{2,1},{3,2},{4,3},{5,4},{6,5},{7,6},{0,7},{9,8},{10,9},{11,1... | collective-permute-start | bytes 12680 | tf_op jit(solution)/shard_map/ppermute | solution.py:21
  94.7 2.9 %collective-permute-done.22 = f32[4,132,2]{2,1,0:T(8,128)S(1)} collective-permute-done((f32[4,132,2]{2,1,0:T(8,128)S(1)}, f32[4,132,2]{2,1,0:T(8,128)S(1)}, u32[]{:S(2)}, u32[]{:S(2)}) %collective-permute-start.22) | collective-permute-done | bytes 4256 | tf_op jit(solution)/shard_map/ppermute | solution.py:21
  99.6 78.8 %psum.7 = f32[64,64]{0,1:T(8,128)S(1)} all-reduce(f32[64,64]{0,1:T(8,128)S(1)} %fusion.12), channel_id=1, replica_groups=mesh['gx'=32,'gy'=8] {'gx','gy'}, use_global_device_ids=true, to_apply=%region_0.0 | all-reduce | flops 4096 | bytes 32768 | tf_op jit(solution)/shard_map/psum | solution.py:84
  178.5 5.8 %cholesky.17 = f32[64,64]{1,0:T(8,128)S(1)} custom-call(f32[64,64]{1,0:T(8,128)S(1)} %fusion.114), custom_call_target="Cholesky" | custom-call | tf_op jit(solution)/shard_map/jit(cholesky)/cholesky | solution.py:85
  185.7 4.9 %custom-call.7 = f32[1,64,64]{1,2,0:T(8,128)S(1)} custom-call(f32[1,64,64]{2,1,0:T(8,128)S(1)} %fusion.112), custom_call_target="InvertDiagBlocksLowerTriangular" | custom-call | tf_op jit(solution)/shard_map/jit(_solve_triangular)/triangular_solve | solution.py:87
  190.9 1.8 fusion
  192.7 4.4 %copy.72 = f32[64,128,128]{2,1,0:T(8,128)} copy(f32[64,128,128]{2,0,1:T(8,128)S(1)} %fusion) | data formatting | bytes 8388608
  (109 shorter events, 23.3 us)
Async XLA Ops:
  1.4 9.6 %collective-permute-start.1 = (f32[4,2,128]{2,1,0:T(2,128)S(1)}, f32[4,2,128]{2,1,0:T(2,128)S(1)}, u32[]{:S(2)}, u32[]{:S(2)}) collective-permute-start(f32[4,2,128]{2,1,0:T(2,128)S(1)} %get-tuple-element.73), channel_id=1, source_target_pairs={{0,8},{8,16},{16,24},{24,32},{32,40},{40,48},{48,56},{56,64},{64,7... | collective-permute-start | bytes 12296 | tf_op jit(solution)/shard_map/ppermute | solution.py:18
  3.9 7.1 %collective-permute-start = (f32[4,2,128]{2,1,0:T(2,128)S(1)}, f32[4,2,128]{2,1,0:T(2,128)S(1)}, u32[]{:S(2)}, u32[]{:S(2)}) collective-permute-start(f32[4,2,128]{2,1,0:T(2,128)S(1)} %get-tuple-element.74), channel_id=1, source_target_pairs={{8,0},{16,8},{24,16},{32,24},{40,32},{48,40},{56,48},{64,56},{72,6... | collective-permute-start | bytes 12296 | tf_op jit(solution)/shard_map/ppermute | solution.py:21
  12.2 7.3 %collective-permute-start.2 = (f32[4,132,2]{2,1,0:T(8,128)S(1)}, f32[4,132,2]{2,1,0:T(8,128)S(1)}, u32[]{:S(2)}, u32[]{:S(2)}) collective-permute-start(f32[4,132,2]{2,1,0:T(8,128)S(1)} %get-tuple-element.60), channel_id=1, source_target_pairs={{1,0},{2,1},{3,2},{4,3},{5,4},{6,5},{7,6},{0,7},{9,8},{10,9},{11,1... | collective-permute-start | bytes 12680 | tf_op jit(solution)/shard_map/ppermute | solution.py:21
  13.7 5.7 %collective-permute-start.3 = (f32[4,132,2]{2,1,0:T(8,128)S(1)}, f32[4,132,2]{2,1,0:T(8,128)S(1)}, u32[]{:S(2)}, u32[]{:S(2)}) collective-permute-start(f32[4,132,2]{2,1,0:T(8,128)S(1)} %get-tuple-element.61), channel_id=1, source_target_pairs={{0,1},{1,2},{2,3},{3,4},{4,5},{5,6},{6,7},{7,0},{8,9},{9,10},{10,1... | collective-permute-start | bytes 12680 | tf_op jit(solution)/shard_map/ppermute | solution.py:18
  21.7 6.2 %collective-permute-start.5 = (f32[4,2,128]{2,1,0:T(2,128)S(1)}, f32[4,2,128]{2,1,0:T(2,128)S(1)}, u32[]{:S(2)}, u32[]{:S(2)}) collective-permute-start(f32[4,2,128]{2,1,0:T(2,128)S(1)} %get-tuple-element.70), channel_id=1, source_target_pairs={{0,8},{8,16},{16,24},{24,32},{32,40},{40,48},{48,56},{56,64},{64,7... | collective-permute-start | bytes 12296 | tf_op jit(solution)/shard_map/ppermute | solution.py:18
  21.8 6.1 %collective-permute-start.4 = (f32[4,2,128]{2,1,0:T(2,128)S(1)}, f32[4,2,128]{2,1,0:T(2,128)S(1)}, u32[]{:S(2)}, u32[]{:S(2)}) collective-permute-start(f32[4,2,128]{2,1,0:T(2,128)S(1)} %get-tuple-element.71), channel_id=1, source_target_pairs={{8,0},{16,8},{24,16},{32,24},{40,32},{48,40},{56,48},{64,56},{72,6... | collective-permute-start | bytes 12296 | tf_op jit(solution)/shard_map/ppermute | solution.py:21
  28.1 6.6 %collective-permute-start.6 = (f32[4,132,2]{2,1,0:T(8,128)S(1)}, f32[4,132,2]{2,1,0:T(8,128)S(1)}, u32[]{:S(2)}, u32[]{:S(2)}) collective-permute-start(f32[4,132,2]{2,1,0:T(8,128)S(1)} %get-tuple-element.58), channel_id=1, source_target_pairs={{1,0},{2,1},{3,2},{4,3},{5,4},{6,5},{7,6},{0,7},{9,8},{10,9},{11,1... | collective-permute-start | bytes 12680 | tf_op jit(solution)/shard_map/ppermute | solution.py:21
  32.0 3.5 %collective-permute-start.7 = (f32[4,132,2]{2,1,0:T(8,128)S(1)}, f32[4,132,2]{2,1,0:T(8,128)S(1)}, u32[]{:S(2)}, u32[]{:S(2)}) collective-permute-start(f32[4,132,2]{2,1,0:T(8,128)S(1)} %get-tuple-element.59), channel_id=1, source_target_pairs={{0,1},{1,2},{2,3},{3,4},{4,5},{5,6},{6,7},{7,0},{8,9},{9,10},{10,1... | collective-permute-start | bytes 12680 | tf_op jit(solution)/shard_map/ppermute | solution.py:18
  36.2 6.1 %collective-permute-start.9 = (f32[4,2,128]{2,1,0:T(2,128)S(1)}, f32[4,2,128]{2,1,0:T(2,128)S(1)}, u32[]{:S(2)}, u32[]{:S(2)}) collective-permute-start(f32[4,2,128]{2,1,0:T(2,128)S(1)} %get-tuple-element.68), channel_id=1, source_target_pairs={{0,8},{8,16},{16,24},{24,32},{32,40},{40,48},{48,56},{56,64},{64,7... | collective-permute-start | bytes 12296 | tf_op jit(solution)/shard_map/ppermute | solution.py:18
  36.3 6.0 %collective-permute-start.8 = (f32[4,2,128]{2,1,0:T(2,128)S(1)}, f32[4,2,128]{2,1,0:T(2,128)S(1)}, u32[]{:S(2)}, u32[]{:S(2)}) collective-permute-start(f32[4,2,128]{2,1,0:T(2,128)S(1)} %get-tuple-element.69), channel_id=1, source_target_pairs={{8,0},{16,8},{24,16},{32,24},{40,32},{48,40},{56,48},{64,56},{72,6... | collective-permute-start | bytes 12296 | tf_op jit(solution)/shard_map/ppermute | solution.py:21
  42.6 7.6 %collective-permute-start.10 = (f32[4,132,2]{2,1,0:T(8,128)S(1)}, f32[4,132,2]{2,1,0:T(8,128)S(1)}, u32[]{:S(2)}, u32[]{:S(2)}) collective-permute-start(f32[4,132,2]{2,1,0:T(8,128)S(1)} %get-tuple-element.56), channel_id=1, source_target_pairs={{1,0},{2,1},{3,2},{4,3},{5,4},{6,5},{7,6},{0,7},{9,8},{10,9},{11,1... | collective-permute-start | bytes 12680 | tf_op jit(solution)/shard_map/ppermute | solution.py:21
  47.1 3.5 %collective-permute-start.11 = (f32[4,132,2]{2,1,0:T(8,128)S(1)}, f32[4,132,2]{2,1,0:T(8,128)S(1)}, u32[]{:S(2)}, u32[]{:S(2)}) collective-permute-start(f32[4,132,2]{2,1,0:T(8,128)S(1)} %get-tuple-element.57), channel_id=1, source_target_pairs={{0,1},{1,2},{2,3},{3,4},{4,5},{5,6},{6,7},{7,0},{8,9},{9,10},{10,1... | collective-permute-start | bytes 12680 | tf_op jit(solution)/shard_map/ppermute | solution.py:18
  51.5 6.2 %collective-permute-start.13 = (f32[4,2,128]{2,1,0:T(2,128)S(1)}, f32[4,2,128]{2,1,0:T(2,128)S(1)}, u32[]{:S(2)}, u32[]{:S(2)}) collective-permute-start(f32[4,2,128]{2,1,0:T(2,128)S(1)} %get-tuple-element.66), channel_id=1, source_target_pairs={{0,8},{8,16},{16,24},{24,32},{32,40},{40,48},{48,56},{56,64},{64,7... | collective-permute-start | bytes 12296 | tf_op jit(solution)/shard_map/ppermute | solution.py:18
  51.5 6.1 %collective-permute-start.12 = (f32[4,2,128]{2,1,0:T(2,128)S(1)}, f32[4,2,128]{2,1,0:T(2,128)S(1)}, u32[]{:S(2)}, u32[]{:S(2)}) collective-permute-start(f32[4,2,128]{2,1,0:T(2,128)S(1)} %get-tuple-element.67), channel_id=1, source_target_pairs={{8,0},{16,8},{24,16},{32,24},{40,32},{48,40},{56,48},{64,56},{72,6... | collective-permute-start | bytes 12296 | tf_op jit(solution)/shard_map/ppermute | solution.py:21
  57.9 7.6 %collective-permute-start.14 = (f32[4,132,2]{2,1,0:T(8,128)S(1)}, f32[4,132,2]{2,1,0:T(8,128)S(1)}, u32[]{:S(2)}, u32[]{:S(2)}) collective-permute-start(f32[4,132,2]{2,1,0:T(8,128)S(1)} %get-tuple-element.54), channel_id=1, source_target_pairs={{1,0},{2,1},{3,2},{4,3},{5,4},{6,5},{7,6},{0,7},{9,8},{10,9},{11,1... | collective-permute-start | bytes 12680 | tf_op jit(solution)/shard_map/ppermute | solution.py:21
  62.5 3.5 %collective-permute-start.15 = (f32[4,132,2]{2,1,0:T(8,128)S(1)}, f32[4,132,2]{2,1,0:T(8,128)S(1)}, u32[]{:S(2)}, u32[]{:S(2)}) collective-permute-start(f32[4,132,2]{2,1,0:T(8,128)S(1)} %get-tuple-element.55), channel_id=1, source_target_pairs={{0,1},{1,2},{2,3},{3,4},{4,5},{5,6},{6,7},{7,0},{8,9},{9,10},{10,1... | collective-permute-start | bytes 12680 | tf_op jit(solution)/shard_map/ppermute | solution.py:18
  66.7 8.5 %collective-permute-start.17 = (f32[4,2,128]{2,1,0:T(2,128)S(1)}, f32[4,2,128]{2,1,0:T(2,128)S(1)}, u32[]{:S(2)}, u32[]{:S(2)}) collective-permute-start(f32[4,2,128]{2,1,0:T(2,128)S(1)} %get-tuple-element.64), channel_id=1, source_target_pairs={{0,8},{8,16},{16,24},{24,32},{32,40},{40,48},{48,56},{56,64},{64,7... | collective-permute-start | bytes 12296 | tf_op jit(solution)/shard_map/ppermute | solution.py:18
  66.8 8.4 %collective-permute-start.16 = (f32[4,2,128]{2,1,0:T(2,128)S(1)}, f32[4,2,128]{2,1,0:T(2,128)S(1)}, u32[]{:S(2)}, u32[]{:S(2)}) collective-permute-start(f32[4,2,128]{2,1,0:T(2,128)S(1)} %get-tuple-element.65), channel_id=1, source_target_pairs={{8,0},{16,8},{24,16},{32,24},{40,32},{48,40},{56,48},{64,56},{72,6... | collective-permute-start | bytes 12296 | tf_op jit(solution)/shard_map/ppermute | solution.py:21
  75.4 7.0 %collective-permute-start.18 = (f32[4,132,2]{2,1,0:T(8,128)S(1)}, f32[4,132,2]{2,1,0:T(8,128)S(1)}, u32[]{:S(2)}, u32[]{:S(2)}) collective-permute-start(f32[4,132,2]{2,1,0:T(8,128)S(1)} %get-tuple-element.52), channel_id=1, source_target_pairs={{1,0},{2,1},{3,2},{4,3},{5,4},{6,5},{7,6},{0,7},{9,8},{10,9},{11,1... | collective-permute-start | bytes 12680 | tf_op jit(solution)/shard_map/ppermute | solution.py:21
  79.4 3.5 %collective-permute-start.19 = (f32[4,132,2]{2,1,0:T(8,128)S(1)}, f32[4,132,2]{2,1,0:T(8,128)S(1)}, u32[]{:S(2)}, u32[]{:S(2)}) collective-permute-start(f32[4,132,2]{2,1,0:T(8,128)S(1)} %get-tuple-element.53), channel_id=1, source_target_pairs={{0,1},{1,2},{2,3},{3,4},{4,5},{5,6},{6,7},{7,0},{8,9},{9,10},{10,1... | collective-permute-start | bytes 12680 | tf_op jit(solution)/shard_map/ppermute | solution.py:18
  83.6 5.9 %collective-permute-start.21 = (f32[4,2,128]{2,1,0:T(2,128)S(1)}, f32[4,2,128]{2,1,0:T(2,128)S(1)}, u32[]{:S(2)}, u32[]{:S(2)}) collective-permute-start(f32[4,2,128]{2,1,0:T(2,128)S(1)} %get-tuple-element.62), channel_id=1, source_target_pairs={{0,8},{8,16},{16,24},{24,32},{32,40},{40,48},{48,56},{56,64},{64,7... | collective-permute-start | bytes 12296 | tf_op jit(solution)/shard_map/ppermute | solution.py:18
  83.7 5.8 %collective-permute-start.20 = (f32[4,2,128]{2,1,0:T(2,128)S(1)}, f32[4,2,128]{2,1,0:T(2,128)S(1)}, u32[]{:S(2)}, u32[]{:S(2)}) collective-permute-start(f32[4,2,128]{2,1,0:T(2,128)S(1)} %get-tuple-element.63), channel_id=1, source_target_pairs={{8,0},{16,8},{24,16},{32,24},{40,32},{48,40},{56,48},{64,56},{72,6... | collective-permute-start | bytes 12296 | tf_op jit(solution)/shard_map/ppermute | solution.py:21
  89.7 7.9 %collective-permute-start.22 = (f32[4,132,2]{2,1,0:T(8,128)S(1)}, f32[4,132,2]{2,1,0:T(8,128)S(1)}, u32[]{:S(2)}, u32[]{:S(2)}) collective-permute-start(f32[4,132,2]{2,1,0:T(8,128)S(1)} %get-tuple-element.50), channel_id=1, source_target_pairs={{1,0},{2,1},{3,2},{4,3},{5,4},{6,5},{7,6},{0,7},{9,8},{10,9},{11,1... | collective-permute-start | bytes 12680 | tf_op jit(solution)/shard_map/ppermute | solution.py:21
  94.5 3.5 %collective-permute-start.23 = (f32[4,132,2]{2,1,0:T(8,128)S(1)}, f32[4,132,2]{2,1,0:T(8,128)S(1)}, u32[]{:S(2)}, u32[]{:S(2)}) collective-permute-start(f32[4,132,2]{2,1,0:T(8,128)S(1)} %get-tuple-element.51), channel_id=1, source_target_pairs={{0,1},{1,2},{2,3},{3,4},{4,5},{5,6},{6,7},{7,0},{8,9},{9,10},{10,1... | collective-permute-start | bytes 12680 | tf_op jit(solution)/shard_map/ppermute | solution.py:18
  (4 other events, 39.1 us)
where the time goes:
time: 197 us
  blocking collectives  78.8 us (40%)
  starting transfers between devices  59.6 us (30%)
  waiting for transfers between devices  25.9 us (13%)
  other arithmetic  19.7 us (10%)
  local copies, waits for them, and re-layouts  9.39 us (5%)
  matrix products  2.72 us (1%)
    psum x1, blocking collectives, body(): gram = lax.psum(local_gram, ('gx', 'gy'))  78.8 us
    ppermute x12, starting transfers between devices, padded_2(): lax.ppermute(lax.slice_in_dim(block, 0, width, axis=dim), axis, backward)  55.4 us
    ppermute x12, waiting for transfers between devices, padded_2(): lax.ppermute(lax.slice_in_dim(block, 0, width, axis=dim), axis, backward)  18.6 us
    unnamed x14, local copies, waits for them, and re-layouts  7.46 us
    ppermute x12, waiting for transfers between devices, padded_2(): lax.ppermute(lax.slice_in_dim(block, block.shape[dim] - width, None, axis...  7.3 us
    another operation x3, other arithmetic, body(): lower_factor = jnp.linalg.cholesky(gram)  6.52 us
    another operation x2, other arithmetic, body(): jax.scipy.linalg.solve_triangular(lower_factor, identity_matrix, lower=True)  5.55 us
    div x6, other arithmetic, derivative_y(): return (8.0 * (ahead_one - behind_one) - (ahead_two - behind_two)) / 12.0  4.75 us
  transfers between devices with their start and end apart: 24, of which 16 were waited for; matrix products, arithmetic and copies ran while one was open for 2% of the time, Pallas kernels for 0%

commit v1 on v0

--- a/solution.py
+++ b/solution.py
@@ -81,7 +81,7 @@
         )
         / cell_total
     )
-    gram = lax.psum(local_gram, ("gx", "gy"))
+    gram = jnp.sum(lax.all_gather(local_gram, ("gx", "gy")), axis=0)
     lower_factor = jnp.linalg.cholesky(gram)
     identity_matrix = jnp.eye(mode_count, dtype=jnp.float32)
     inverse = jax.scipy.linalg.solve_triangular(lower_factor, identity_matrix, lower=True)

time: 197 us -> 253 us (1.28)
  waiting for transfers between devices: 25.9 us -> 159 us
  blocking collectives: 78.8 us -> 0 us
  starting transfers between devices: 59.6 us -> 43 us
  between operations: 1.17 us -> 14.5 us
  other arithmetic: 19.7 us -> 23.8 us
    all_gather x0 -> x1, waiting for transfers between devices: none -> 111 us  [body(): gram = jnp.sum(lax.all_gather(local_gram, ('gx', 'gy')), axis=0)]
    psum x1 -> x0, blocking collectives: 78.8 us -> none  [body(): gram = lax.psum(local_gram, ('gx', 'gy'))]
    ppermute x12, starting transfers between devices: 55.4 us -> 34.5 us  [padded_2(): lax.ppermute(lax.slice_in_dim(block, 0, width, axis=dim), axis, backward)]
    ppermute x12, waiting for transfers between devices: 7.3 us -> 24.2 us  [padded_2(): lax.ppermute(lax.slice_in_dim(block, block.shape[dim] - width, None, axis...]
    ppermute x12, waiting for transfers between devices: 18.6 us -> 23.7 us  [padded_2(): lax.ppermute(lax.slice_in_dim(block, 0, width, axis=dim), axis, backward)]
    ppermute x12, starting transfers between devices: 4.12 us -> 8.5 us  [padded_2(): lax.ppermute(lax.slice_in_dim(block, block.shape[dim] - width, None, axis...]
    reduce_sum x0 -> x1, other arithmetic: none -> 4.01 us  [body(): gram = jnp.sum(lax.all_gather(local_gram, ('gx', 'gy')), axis=0)]
  transfers between devices with their start and end apart: 24 -> 25, of which waited for: 16 -> 23; matrix products, arithmetic and copies ran while one was open for 2% -> 1% of each run, Pallas kernels for 0% -> 0%
where the time goes in v1:
time: 253 us
  waiting for transfers between devices  159 us (63%)
  starting transfers between devices  43 us (17%)
  other arithmetic  23.8 us (9%)
  between operations  14.5 us (6%)
  local copies, waits for them, and re-layouts  9.28 us (4%)
  matrix products  3.33 us (1%)
    all_gather x1, waiting for transfers between devices, body(): gram = jnp.sum(lax.all_gather(local_gram, ('gx', 'gy')), axis=0)  111 us
    ppermute x12, starting transfers between devices, padded_2(): lax.ppermute(lax.slice_in_dim(block, 0, width, axis=dim), axis, backward)  34.5 us
    ppermute x12, waiting for transfers between devices, padded_2(): lax.ppermute(lax.slice_in_dim(block, block.shape[dim] - width, None, axis...  24.2 us
    ppermute x12, waiting for transfers between devices, padded_2(): lax.ppermute(lax.slice_in_dim(block, 0, width, axis=dim), axis, backward)  23.7 us
    ppermute x12, starting transfers between devices, padded_2(): lax.ppermute(lax.slice_in_dim(block, block.shape[dim] - width, None, axis...  8.5 us
    unnamed x14, local copies, waits for them, and re-layouts  7.36 us
    another operation x3, other arithmetic, body(): lower_factor = jnp.linalg.cholesky(gram)  6.52 us
    another operation x2, other arithmetic, body(): jax.scipy.linalg.solve_triangular(lower_factor, identity_matrix, lower=True)  5.55 us
  transfers between devices with their start and end apart: 25, of which 23 were waited for; matrix products, arithmetic and copies ran while one was open for 1% of the time, Pallas kernels for 0%

profile of v1, /device:TPU:1, one launch (start us, length us, event | category | flops | bytes accessed | tf_op | source)
XLA Modules:
  0.0 252.8 jit_solution(4214853314148689613)
XLA Ops:
  8.0 8.6 %collective-permute-start = (f32[4,2,128]{2,1,0:T(2,128)S(1)}, f32[4,2,128]{2,1,0:T(2,128)S(1)}, u32[]{:S(2)}, u32[]{:S(2)}) collective-permute-start(f32[4,2,128]{2,1,0:T(2,128)S(1)} %get-tuple-element.76), channel_id=1, source_target_pairs={{8,0},{16,8},{24,16},{32,24},{40,32},{48,40},{56,48},{64,56},{72,6... | collective-permute-start | bytes 12296 | tf_op jit(solution)/shard_map/ppermute | solution.py:21
  17.4 5.0 %collective-permute-done.1 = f32[4,2,128]{2,1,0:T(2,128)S(1)} collective-permute-done((f32[4,2,128]{2,1,0:T(2,128)S(1)}, f32[4,2,128]{2,1,0:T(2,128)S(1)}, u32[]{:S(2)}, u32[]{:S(2)}) %collective-permute-start.1) | collective-permute-done | bytes 4128 | tf_op jit(solution)/shard_map/ppermute | solution.py:18
  23.5 2.1 collective-permute-start.2
  26.8 4.5 %collective-permute-done.2 = f32[4,132,2]{2,1,0:T(8,128)S(1)} collective-permute-done((f32[4,132,2]{2,1,0:T(8,128)S(1)}, f32[4,132,2]{2,1,0:T(8,128)S(1)}, u32[]{:S(2)}, u32[]{:S(2)}) %collective-permute-start.2) | collective-permute-done | bytes 4256 | tf_op jit(solution)/shard_map/ppermute | solution.py:21
  36.3 3.4 %collective-permute-done.5 = f32[4,2,128]{2,1,0:T(2,128)S(1)} collective-permute-done((f32[4,2,128]{2,1,0:T(2,128)S(1)}, f32[4,2,128]{2,1,0:T(2,128)S(1)}, u32[]{:S(2)}, u32[]{:S(2)}) %collective-permute-start.5) | collective-permute-done | bytes 4128 | tf_op jit(solution)/shard_map/ppermute | solution.py:18
  39.8 3.8 %collective-permute-start.6 = (f32[4,132,2]{2,1,0:T(8,128)S(1)}, f32[4,132,2]{2,1,0:T(8,128)S(1)}, u32[]{:S(2)}, u32[]{:S(2)}) collective-permute-start(f32[4,132,2]{2,1,0:T(8,128)S(1)} %get-tuple-element.60), channel_id=1, source_target_pairs={{1,0},{2,1},{3,2},{4,3},{5,4},{6,5},{7,6},{0,7},{9,8},{10,9},{11,1... | collective-permute-start | bytes 12680 | tf_op jit(solution)/shard_map/ppermute | solution.py:21
  43.8 2.9 %collective-permute-done.6 = f32[4,132,2]{2,1,0:T(8,128)S(1)} collective-permute-done((f32[4,132,2]{2,1,0:T(8,128)S(1)}, f32[4,132,2]{2,1,0:T(8,128)S(1)}, u32[]{:S(2)}, u32[]{:S(2)}) %collective-permute-start.6) | collective-permute-done | bytes 4256 | tf_op jit(solution)/shard_map/ppermute | solution.py:21
  50.5 3.4 %collective-permute-done.9 = f32[4,2,128]{2,1,0:T(2,128)S(1)} collective-permute-done((f32[4,2,128]{2,1,0:T(2,128)S(1)}, f32[4,2,128]{2,1,0:T(2,128)S(1)}, u32[]{:S(2)}, u32[]{:S(2)}) %collective-permute-start.9) | collective-permute-done | bytes 4128 | tf_op jit(solution)/shard_map/ppermute | solution.py:18
  54.1 4.9 %collective-permute-start.10 = (f32[4,132,2]{2,1,0:T(8,128)S(1)}, f32[4,132,2]{2,1,0:T(8,128)S(1)}, u32[]{:S(2)}, u32[]{:S(2)}) collective-permute-start(f32[4,132,2]{2,1,0:T(8,128)S(1)} %get-tuple-element.58), channel_id=1, source_target_pairs={{1,0},{2,1},{3,2},{4,3},{5,4},{6,5},{7,6},{0,7},{9,8},{10,9},{11,1... | collective-permute-start | bytes 12680 | tf_op jit(solution)/shard_map/ppermute | solution.py:21
  59.1 2.9 %collective-permute-done.10 = f32[4,132,2]{2,1,0:T(8,128)S(1)} collective-permute-done((f32[4,132,2]{2,1,0:T(8,128)S(1)}, f32[4,132,2]{2,1,0:T(8,128)S(1)}, u32[]{:S(2)}, u32[]{:S(2)}) %collective-permute-start.10) | collective-permute-done | bytes 4256 | tf_op jit(solution)/shard_map/ppermute | solution.py:21
  65.8 3.4 %collective-permute-done.13 = f32[4,2,128]{2,1,0:T(2,128)S(1)} collective-permute-done((f32[4,2,128]{2,1,0:T(2,128)S(1)}, f32[4,2,128]{2,1,0:T(2,128)S(1)}, u32[]{:S(2)}, u32[]{:S(2)}) %collective-permute-start.13) | collective-permute-done | bytes 4128 | tf_op jit(solution)/shard_map/ppermute | solution.py:18
  69.3 4.9 %collective-permute-start.14 = (f32[4,132,2]{2,1,0:T(8,128)S(1)}, f32[4,132,2]{2,1,0:T(8,128)S(1)}, u32[]{:S(2)}, u32[]{:S(2)}) collective-permute-start(f32[4,132,2]{2,1,0:T(8,128)S(1)} %get-tuple-element.56), channel_id=1, source_target_pairs={{1,0},{2,1},{3,2},{4,3},{5,4},{6,5},{7,6},{0,7},{9,8},{10,9},{11,1... | collective-permute-start | bytes 12680 | tf_op jit(solution)/shard_map/ppermute | solution.py:21
  74.3 2.9 %collective-permute-done.14 = f32[4,132,2]{2,1,0:T(8,128)S(1)} collective-permute-done((f32[4,132,2]{2,1,0:T(8,128)S(1)}, f32[4,132,2]{2,1,0:T(8,128)S(1)}, u32[]{:S(2)}, u32[]{:S(2)}) %collective-permute-start.14) | collective-permute-done | bytes 4256 | tf_op jit(solution)/shard_map/ppermute | solution.py:21
  81.0 3.5 %collective-permute-done.17 = f32[4,2,128]{2,1,0:T(2,128)S(1)} collective-permute-done((f32[4,2,128]{2,1,0:T(2,128)S(1)}, f32[4,2,128]{2,1,0:T(2,128)S(1)}, u32[]{:S(2)}, u32[]{:S(2)}) %collective-permute-start.17) | collective-permute-done | bytes 4128 | tf_op jit(solution)/shard_map/ppermute | solution.py:18
  84.8 4.9 %collective-permute-start.18 = (f32[4,132,2]{2,1,0:T(8,128)S(1)}, f32[4,132,2]{2,1,0:T(8,128)S(1)}, u32[]{:S(2)}, u32[]{:S(2)}) collective-permute-start(f32[4,132,2]{2,1,0:T(8,128)S(1)} %get-tuple-element.54), channel_id=1, source_target_pairs={{1,0},{2,1},{3,2},{4,3},{5,4},{6,5},{7,6},{0,7},{9,8},{10,9},{11,1... | collective-permute-start | bytes 12680 | tf_op jit(solution)/shard_map/ppermute | solution.py:21
  89.8 2.9 %collective-permute-done.18 = f32[4,132,2]{2,1,0:T(8,128)S(1)} collective-permute-done((f32[4,132,2]{2,1,0:T(8,128)S(1)}, f32[4,132,2]{2,1,0:T(8,128)S(1)}, u32[]{:S(2)}, u32[]{:S(2)}) %collective-permute-start.18) | collective-permute-done | bytes 4256 | tf_op jit(solution)/shard_map/ppermute | solution.py:21
  96.8 3.0 %collective-permute-done.21 = f32[4,2,128]{2,1,0:T(2,128)S(1)} collective-permute-done((f32[4,2,128]{2,1,0:T(2,128)S(1)}, f32[4,2,128]{2,1,0:T(2,128)S(1)}, u32[]{:S(2)}, u32[]{:S(2)}) %collective-permute-start.21) | collective-permute-done | bytes 4128 | tf_op jit(solution)/shard_map/ppermute | solution.py:18
  100.0 4.9 %collective-permute-start.22 = (f32[4,132,2]{2,1,0:T(8,128)S(1)}, f32[4,132,2]{2,1,0:T(8,128)S(1)}, u32[]{:S(2)}, u32[]{:S(2)}) collective-permute-start(f32[4,132,2]{2,1,0:T(8,128)S(1)} %get-tuple-element.52), channel_id=1, source_target_pairs={{1,0},{2,1},{3,2},{4,3},{5,4},{6,5},{7,6},{0,7},{9,8},{10,9},{11,1... | collective-permute-start | bytes 12680 | tf_op jit(solution)/shard_map/ppermute | solution.py:21
  105.0 2.9 %collective-permute-done.22 = f32[4,132,2]{2,1,0:T(8,128)S(1)} collective-permute-done((f32[4,132,2]{2,1,0:T(8,128)S(1)}, f32[4,132,2]{2,1,0:T(8,128)S(1)}, u32[]{:S(2)}, u32[]{:S(2)}) %collective-permute-start.22) | collective-permute-done | bytes 4256 | tf_op jit(solution)/shard_map/ppermute | solution.py:21
  112.3 111.0 %all-gather.3.cloned.1.call-done = f32[16384,64]{1,0:T(8,128)} async-done(((f32[64,64]{1,0:T(8,128)}), f32[16384,64]{1,0:T(8,128)}) %all-gather.3.cloned.1.call-update) | async-done | bytes 4194320 | tf_op jit(solution)/shard_map/all_gather | solution.py:84
  223.3 4.0 %reduce_sum.9 = f32[64,64]{1,0:T(8,128)S(1)} reduce(f32[256,64,64]{2,1,0:T(8,128)} %bitcast.121, f32[]{:T(128)} %constant.85.clone.1), dimensions={0}, to_apply=%region_0.0 | reduce | flops 1044480 | bytes 4210692 | tf_op jit(solution)/shard_map/reduce_sum | solution.py:84
  227.4 5.8 %cholesky.17 = f32[64,64]{1,0:T(8,128)S(1)} custom-call(f32[64,64]{1,0:T(8,128)S(1)} %fusion.114), custom_call_target="Cholesky" | custom-call | tf_op jit(solution)/shard_map/jit(cholesky)/cholesky | solution.py:85
  234.6 4.9 %custom-call.7 = f32[1,64,64]{1,2,0:T(8,128)S(1)} custom-call(f32[1,64,64]{2,1,0:T(8,128)S(1)} %fusion.112), custom_call_target="InvertDiagBlocksLowerTriangular" | custom-call | tf_op jit(solution)/shard_map/jit(_solve_triangular)/triangular_solve | solution.py:87
  241.5 4.4 %copy.99 = f32[64,128,128]{2,1,0:T(8,128)} copy(f32[64,128,128]{2,0,1:T(8,128)S(1)} %fusion) | data formatting | bytes 8388608
  (112 shorter events, 33.4 us)
Async XLA Ops:
  7.2 216.1 %all-gather.3.cloned.1.call-start = ((), (), s32[]{:S(2)}) async-start(), calls=%async_computation | async-start | bytes 8421376 | tf_op jit(solution)/shard_map/all_gather | solution.py:84
  8.0 9.4 %collective-permute-start = (f32[4,2,128]{2,1,0:T(2,128)S(1)}, f32[4,2,128]{2,1,0:T(2,128)S(1)}, u32[]{:S(2)}, u32[]{:S(2)}) collective-permute-start(f32[4,2,128]{2,1,0:T(2,128)S(1)} %get-tuple-element.76), channel_id=1, source_target_pairs={{8,0},{16,8},{24,16},{32,24},{40,32},{48,40},{56,48},{64,56},{72,6... | collective-permute-start | bytes 12296 | tf_op jit(solution)/shard_map/ppermute | solution.py:21
  16.6 5.8 %collective-permute-start.1 = (f32[4,2,128]{2,1,0:T(2,128)S(1)}, f32[4,2,128]{2,1,0:T(2,128)S(1)}, u32[]{:S(2)}, u32[]{:S(2)}) collective-permute-start(f32[4,2,128]{2,1,0:T(2,128)S(1)} %get-tuple-element.75), channel_id=1, source_target_pairs={{0,8},{8,16},{16,24},{24,32},{32,40},{40,48},{48,56},{56,64},{64,7... | collective-permute-start | bytes 12296 | tf_op jit(solution)/shard_map/ppermute | solution.py:18
  23.5 7.8 %collective-permute-start.2 = (f32[4,132,2]{2,1,0:T(8,128)S(1)}, f32[4,132,2]{2,1,0:T(8,128)S(1)}, u32[]{:S(2)}, u32[]{:S(2)}) collective-permute-start(f32[4,132,2]{2,1,0:T(8,128)S(1)} %get-tuple-element.62), channel_id=1, source_target_pairs={{1,0},{2,1},{3,2},{4,3},{5,4},{6,5},{7,6},{0,7},{9,8},{10,9},{11,1... | collective-permute-start | bytes 12680 | tf_op jit(solution)/shard_map/ppermute | solution.py:21
  25.6 5.7 %collective-permute-start.3 = (f32[4,132,2]{2,1,0:T(8,128)S(1)}, f32[4,132,2]{2,1,0:T(8,128)S(1)}, u32[]{:S(2)}, u32[]{:S(2)}) collective-permute-start(f32[4,132,2]{2,1,0:T(8,128)S(1)} %get-tuple-element.63), channel_id=1, source_target_pairs={{0,1},{1,2},{2,3},{3,4},{4,5},{5,6},{6,7},{7,0},{8,9},{9,10},{10,1... | collective-permute-start | bytes 12680 | tf_op jit(solution)/shard_map/ppermute | solution.py:18
  33.7 2.5 %collective-permute-start.4 = (f32[4,2,128]{2,1,0:T(2,128)S(1)}, f32[4,2,128]{2,1,0:T(2,128)S(1)}, u32[]{:S(2)}, u32[]{:S(2)}) collective-permute-start(f32[4,2,128]{2,1,0:T(2,128)S(1)} %get-tuple-element.73), channel_id=1, source_target_pairs={{8,0},{16,8},{24,16},{32,24},{40,32},{48,40},{56,48},{64,56},{72,6... | collective-permute-start | bytes 12296 | tf_op jit(solution)/shard_map/ppermute | solution.py:21
  33.8 5.9 %collective-permute-start.5 = (f32[4,2,128]{2,1,0:T(2,128)S(1)}, f32[4,2,128]{2,1,0:T(2,128)S(1)}, u32[]{:S(2)}, u32[]{:S(2)}) collective-permute-start(f32[4,2,128]{2,1,0:T(2,128)S(1)} %get-tuple-element.72), channel_id=1, source_target_pairs={{0,8},{8,16},{16,24},{24,32},{32,40},{40,48},{48,56},{56,64},{64,7... | collective-permute-start | bytes 12296 | tf_op jit(solution)/shard_map/ppermute | solution.py:18
  39.8 6.9 %collective-permute-start.6 = (f32[4,132,2]{2,1,0:T(8,128)S(1)}, f32[4,132,2]{2,1,0:T(8,128)S(1)}, u32[]{:S(2)}, u32[]{:S(2)}) collective-permute-start(f32[4,132,2]{2,1,0:T(8,128)S(1)} %get-tuple-element.60), channel_id=1, source_target_pairs={{1,0},{2,1},{3,2},{4,3},{5,4},{6,5},{7,6},{0,7},{9,8},{10,9},{11,1... | collective-permute-start | bytes 12680 | tf_op jit(solution)/shard_map/ppermute | solution.py:21
  43.7 3.5 %collective-permute-start.7 = (f32[4,132,2]{2,1,0:T(8,128)S(1)}, f32[4,132,2]{2,1,0:T(8,128)S(1)}, u32[]{:S(2)}, u32[]{:S(2)}) collective-permute-start(f32[4,132,2]{2,1,0:T(8,128)S(1)} %get-tuple-element.61), channel_id=1, source_target_pairs={{0,1},{1,2},{2,3},{3,4},{4,5},{5,6},{6,7},{7,0},{8,9},{9,10},{10,1... | collective-permute-start | bytes 12680 | tf_op jit(solution)/shard_map/ppermute | solution.py:18
  47.9 2.6 %collective-permute-start.8 = (f32[4,2,128]{2,1,0:T(2,128)S(1)}, f32[4,2,128]{2,1,0:T(2,128)S(1)}, u32[]{:S(2)}, u32[]{:S(2)}) collective-permute-start(f32[4,2,128]{2,1,0:T(2,128)S(1)} %get-tuple-element.71), channel_id=1, source_target_pairs={{8,0},{16,8},{24,16},{32,24},{40,32},{48,40},{56,48},{64,56},{72,6... | collective-permute-start | bytes 12296 | tf_op jit(solution)/shard_map/ppermute | solution.py:21
  48.0 5.9 %collective-permute-start.9 = (f32[4,2,128]{2,1,0:T(2,128)S(1)}, f32[4,2,128]{2,1,0:T(2,128)S(1)}, u32[]{:S(2)}, u32[]{:S(2)}) collective-permute-start(f32[4,2,128]{2,1,0:T(2,128)S(1)} %get-tuple-element.70), channel_id=1, source_target_pairs={{0,8},{8,16},{16,24},{24,32},{32,40},{40,48},{48,56},{56,64},{64,7... | collective-permute-start | bytes 12296 | tf_op jit(solution)/shard_map/ppermute | solution.py:18
  54.1 7.9 %collective-permute-start.10 = (f32[4,132,2]{2,1,0:T(8,128)S(1)}, f32[4,132,2]{2,1,0:T(8,128)S(1)}, u32[]{:S(2)}, u32[]{:S(2)}) collective-permute-start(f32[4,132,2]{2,1,0:T(8,128)S(1)} %get-tuple-element.58), channel_id=1, source_target_pairs={{1,0},{2,1},{3,2},{4,3},{5,4},{6,5},{7,6},{0,7},{9,8},{10,9},{11,1... | collective-permute-start | bytes 12680 | tf_op jit(solution)/shard_map/ppermute | solution.py:21
  58.9 3.5 %collective-permute-start.11 = (f32[4,132,2]{2,1,0:T(8,128)S(1)}, f32[4,132,2]{2,1,0:T(8,128)S(1)}, u32[]{:S(2)}, u32[]{:S(2)}) collective-permute-start(f32[4,132,2]{2,1,0:T(8,128)S(1)} %get-tuple-element.59), channel_id=1, source_target_pairs={{0,1},{1,2},{2,3},{3,4},{4,5},{5,6},{6,7},{7,0},{8,9},{9,10},{10,1... | collective-permute-start | bytes 12680 | tf_op jit(solution)/shard_map/ppermute | solution.py:18
  63.3 5.9 %collective-permute-start.13 = (f32[4,2,128]{2,1,0:T(2,128)S(1)}, f32[4,2,128]{2,1,0:T(2,128)S(1)}, u32[]{:S(2)}, u32[]{:S(2)}) collective-permute-start(f32[4,2,128]{2,1,0:T(2,128)S(1)} %get-tuple-element.68), channel_id=1, source_target_pairs={{0,8},{8,16},{16,24},{24,32},{32,40},{40,48},{48,56},{56,64},{64,7... | collective-permute-start | bytes 12296 | tf_op jit(solution)/shard_map/ppermute | solution.py:18
  69.3 7.9 %collective-permute-start.14 = (f32[4,132,2]{2,1,0:T(8,128)S(1)}, f32[4,132,2]{2,1,0:T(8,128)S(1)}, u32[]{:S(2)}, u32[]{:S(2)}) collective-permute-start(f32[4,132,2]{2,1,0:T(8,128)S(1)} %get-tuple-element.56), channel_id=1, source_target_pairs={{1,0},{2,1},{3,2},{4,3},{5,4},{6,5},{7,6},{0,7},{9,8},{10,9},{11,1... | collective-permute-start | bytes 12680 | tf_op jit(solution)/shard_map/ppermute | solution.py:21
  74.2 3.5 %collective-permute-start.15 = (f32[4,132,2]{2,1,0:T(8,128)S(1)}, f32[4,132,2]{2,1,0:T(8,128)S(1)}, u32[]{:S(2)}, u32[]{:S(2)}) collective-permute-start(f32[4,132,2]{2,1,0:T(8,128)S(1)} %get-tuple-element.57), channel_id=1, source_target_pairs={{0,1},{1,2},{2,3},{3,4},{4,5},{5,6},{6,7},{7,0},{8,9},{9,10},{10,1... | collective-permute-start | bytes 12680 | tf_op jit(solution)/shard_map/ppermute | solution.py:18
  78.5 2.6 %collective-permute-start.16 = (f32[4,2,128]{2,1,0:T(2,128)S(1)}, f32[4,2,128]{2,1,0:T(2,128)S(1)}, u32[]{:S(2)}, u32[]{:S(2)}) collective-permute-start(f32[4,2,128]{2,1,0:T(2,128)S(1)} %get-tuple-element.67), channel_id=1, source_target_pairs={{8,0},{16,8},{24,16},{32,24},{40,32},{48,40},{56,48},{64,56},{72,6... | collective-permute-start | bytes 12296 | tf_op jit(solution)/shard_map/ppermute | solution.py:21
  78.5 6.0 %collective-permute-start.17 = (f32[4,2,128]{2,1,0:T(2,128)S(1)}, f32[4,2,128]{2,1,0:T(2,128)S(1)}, u32[]{:S(2)}, u32[]{:S(2)}) collective-permute-start(f32[4,2,128]{2,1,0:T(2,128)S(1)} %get-tuple-element.66), channel_id=1, source_target_pairs={{0,8},{8,16},{16,24},{24,32},{32,40},{40,48},{48,56},{56,64},{64,7... | collective-permute-start | bytes 12296 | tf_op jit(solution)/shard_map/ppermute | solution.py:18
  84.8 7.9 %collective-permute-start.18 = (f32[4,132,2]{2,1,0:T(8,128)S(1)}, f32[4,132,2]{2,1,0:T(8,128)S(1)}, u32[]{:S(2)}, u32[]{:S(2)}) collective-permute-start(f32[4,132,2]{2,1,0:T(8,128)S(1)} %get-tuple-element.54), channel_id=1, source_target_pairs={{1,0},{2,1},{3,2},{4,3},{5,4},{6,5},{7,6},{0,7},{9,8},{10,9},{11,1... | collective-permute-start | bytes 12680 | tf_op jit(solution)/shard_map/ppermute | solution.py:21
  89.6 3.5 %collective-permute-start.19 = (f32[4,132,2]{2,1,0:T(8,128)S(1)}, f32[4,132,2]{2,1,0:T(8,128)S(1)}, u32[]{:S(2)}, u32[]{:S(2)}) collective-permute-start(f32[4,132,2]{2,1,0:T(8,128)S(1)} %get-tuple-element.55), channel_id=1, source_target_pairs={{0,1},{1,2},{2,3},{3,4},{4,5},{5,6},{6,7},{7,0},{8,9},{9,10},{10,1... | collective-permute-start | bytes 12680 | tf_op jit(solution)/shard_map/ppermute | solution.py:18
  93.9 2.9 %collective-permute-start.20 = (f32[4,2,128]{2,1,0:T(2,128)S(1)}, f32[4,2,128]{2,1,0:T(2,128)S(1)}, u32[]{:S(2)}, u32[]{:S(2)}) collective-permute-start(f32[4,2,128]{2,1,0:T(2,128)S(1)} %get-tuple-element.65), channel_id=1, source_target_pairs={{8,0},{16,8},{24,16},{32,24},{40,32},{48,40},{56,48},{64,56},{72,6... | collective-permute-start | bytes 12296 | tf_op jit(solution)/shard_map/ppermute | solution.py:21
  94.0 5.9 %collective-permute-start.21 = (f32[4,2,128]{2,1,0:T(2,128)S(1)}, f32[4,2,128]{2,1,0:T(2,128)S(1)}, u32[]{:S(2)}, u32[]{:S(2)}) collective-permute-start(f32[4,2,128]{2,1,0:T(2,128)S(1)} %get-tuple-element.64), channel_id=1, source_target_pairs={{0,8},{8,16},{16,24},{24,32},{32,40},{40,48},{48,56},{56,64},{64,7... | collective-permute-start | bytes 12296 | tf_op jit(solution)/shard_map/ppermute | solution.py:18
  100.0 7.9 %collective-permute-start.22 = (f32[4,132,2]{2,1,0:T(8,128)S(1)}, f32[4,132,2]{2,1,0:T(8,128)S(1)}, u32[]{:S(2)}, u32[]{:S(2)}) collective-permute-start(f32[4,132,2]{2,1,0:T(8,128)S(1)} %get-tuple-element.52), channel_id=1, source_target_pairs={{1,0},{2,1},{3,2},{4,3},{5,4},{6,5},{7,6},{0,7},{9,8},{10,9},{11,1... | collective-permute-start | bytes 12680 | tf_op jit(solution)/shard_map/ppermute | solution.py:21
  104.9 3.5 %collective-permute-start.23 = (f32[4,132,2]{2,1,0:T(8,128)S(1)}, f32[4,132,2]{2,1,0:T(8,128)S(1)}, u32[]{:S(2)}, u32[]{:S(2)}) collective-permute-start(f32[4,132,2]{2,1,0:T(8,128)S(1)} %get-tuple-element.53), channel_id=1, source_target_pairs={{0,1},{1,2},{2,3},{3,4},{4,5},{5,6},{6,7},{7,0},{8,9},{9,10},{10,1... | collective-permute-start | bytes 12680 | tf_op jit(solution)/shard_map/ppermute | solution.py:18
  (5 other events, 45.5 us)
Sparse Core Ops, SparseCore 0:
  110.7 112.5 all-gather.2
